TPU v7x, 128 devices: a whole 4x4x4 slice. The times are simulated.
128 devices in a mesh: shot: 4 (over z_hi, core), gx: 16 (over x, y), gy: 2 (over z_lo).
Axes of the slice: x: 4, y: 4, z: 4 (z_hi: 2, z_lo: 2; z = z_hi * 2 + z_lo), core: 2. Of those that a mesh axis runs over, the one named last changes fastest.
Arguments:
- wave_now: float32 [4, 4, 512, 64, 128], P('shot', None, 'gx', 'gy'), may hold values from -6 to 6
- wave_prev: float32 [4, 4, 512, 64, 128], P('shot', None, 'gx', 'gy'), may hold values from -6 to 6
- vel_coef: float32 [512, 64, 128], P('gx', 'gy'), may hold values from 0.08 to 0.18
- epsilon: float32 [512, 64, 128], P('gx', 'gy'), may hold values from 0.15 to 0.35
- delta: float32 [512, 64, 128], P('gx', 'gy'), may hold values from 0 to 0.15
- tilt: int32 [512, 64, 128], P('gx', 'gy'), may hold values from 0 to 60
- azimuth: int32 [512, 64, 128], P('gx', 'gy'), may hold values from 0 to 359
- aperture: int32 [4, 16, 2], P('shot', 'gx', 'gy'), may hold values 0 or 1
Outputs:
- wave_final: float32 [4, 4, 512, 64, 128], P('shot', None, 'gx', 'gy')
- image: float32 [512, 64, 128], P('gx', 'gy')
All inputs are finite; a program needn't handle non-finite values. No bound on the sum of `aperture` on one device may be relied on, other than what follows from the above.
Results may differ from a plain program's by a relative error of at most 0.00002.
Values sent between devices are 32-bit elements; how exact they have to be, the bound alone decides.
A program may use at most 128 MiB of HBM per device.

v0:
```python
import math
import jax
import jax.numpy as jnp
from jax import lax
from jax.sharding import PartitionSpec as P

ITERS = 4


def extended(block, sides, width):
    for axis, dim in sides:
        count = lax.axis_size(axis)
        forward = [(i, i + 1) for i in range(count - 1)]
        backward = [(target, source) for source, target in forward]
        low = lax.ppermute(
            lax.slice_in_dim(block, block.shape[dim] - width, None, axis=dim), axis, forward
        )
        high = lax.ppermute(lax.slice_in_dim(block, 0, width, axis=dim), axis, backward)
        block = jnp.concatenate([low, block, high], axis=dim)
    return block


def model_terms(vel_coef, epsilon, delta, tilt, azimuth):
    theta = tilt.astype(jnp.float32) * (math.pi / 180.0)
    phi = azimuth.astype(jnp.float32) * (math.pi / 180.0)
    normal_x = jnp.sin(theta) * jnp.cos(phi)
    normal_y = jnp.sin(theta) * jnp.sin(phi)
    normal_z = jnp.cos(theta)
    gain = 1.0 + 2.0 * epsilon
    root = jnp.sqrt(1.0 + 2.0 * delta)
    return jnp.stack([normal_x, normal_y, normal_z, vel_coef, gain, root], axis=0)


def advance(padded, previous, coef):
    width_x = padded.shape[-3] - 2
    width_y = padded.shape[-2] - 2
    width_z = padded.shape[-1] - 2

    def shifted(off_x, off_y, off_z):
        return padded[
            ...,
            1 + off_x : 1 + off_x + width_x,
            1 + off_y : 1 + off_y + width_y,
            1 + off_z : 1 + off_z + width_z,
        ]

    centre = shifted(0, 0, 0)
    second_x = shifted(1, 0, 0) + shifted(-1, 0, 0) - 2.0 * centre
    second_y = shifted(0, 1, 0) + shifted(0, -1, 0) - 2.0 * centre
    second_z = shifted(0, 0, 1) + shifted(0, 0, -1) - 2.0 * centre
    mixed_xy = 0.25 * (
        shifted(1, 1, 0) - shifted(1, -1, 0) - shifted(-1, 1, 0) + shifted(-1, -1, 0)
    )
    mixed_xz = 0.25 * (
        shifted(1, 0, 1) - shifted(1, 0, -1) - shifted(-1, 0, 1) + shifted(-1, 0, -1)
    )
    mixed_yz = 0.25 * (
        shifted(0, 1, 1) - shifted(0, 1, -1) - shifted(0, -1, 1) + shifted(0, -1, -1)
    )
    normal_x, normal_y, normal_z = (coef[0], coef[1], coef[2])
    speed, gain, root = (coef[3], coef[4], coef[5])
    along = (
        normal_x * normal_x * second_x
        + normal_y * normal_y * second_y
        + normal_z * normal_z * second_z
        + 2.0
        * (
            normal_x * normal_y * mixed_xy
            + normal_x * normal_z * mixed_xz
            + normal_y * normal_z * mixed_yz
        )
    )
    across = second_x + second_y + second_z - along
    pressure = centre[:, 0::2]
    auxiliary = centre[:, 1::2]
    rhs_p = gain * across[:, 0::2] + root * along[:, 1::2]
    rhs_q = root * across[:, 0::2] + along[:, 1::2]
    next_p = 2.0 * pressure - previous[:, 0::2] + speed * rhs_p
    next_q = 2.0 * auxiliary - previous[:, 1::2] + speed * rhs_q
    return jnp.stack([next_p, next_q], axis=2).reshape(centre.shape)


def depth_pad(array):
    return jnp.pad(array, ((0, 0), (0, 0), (0, 0), (0, 0), (1, 1)))


def local(wave_now, wave_prev, vel_coef, epsilon, delta, tilt, azimuth, aperture):
    coef = model_terms(vel_coef, epsilon, delta, tilt, azimuth)
    correlation = jnp.zeros(vel_coef.shape, jnp.float32)
    current, previous = (wave_now, wave_prev)
    for step in range(ITERS):
        widened_now = extended(current, (("gx", 2), ("gy", 3)), 1)
        fresh = advance(depth_pad(widened_now), previous, coef)
        correlation = correlation + fresh[0, 0] * fresh[0, 2]
        previous, current = (current, fresh)
    covered = aperture[0, 0, 0].astype(jnp.float32)
    image = lax.psum(covered * correlation, "shot") / ITERS
    return (current, image)


def solution(mesh):
    return jax.shard_map(
        local,
        mesh=mesh,
        in_specs=(
            P("shot", None, "gx", "gy", None),
            P("shot", None, "gx", "gy", None),
            P("gx", "gy", None),
            P("gx", "gy", None),
            P("gx", "gy", None),
            P("gx", "gy", None),
            P("gx", "gy", None),
            P("shot", "gx", "gy"),
        ),
        out_specs=(P("shot", None, "gx", "gy", None), P("gx", "gy", None)),
        check_vma=False,
    )
```

profile of v0, /device:TPU:1, one launch (start us, length us, event | category | flops | bytes accessed | tf_op | source)
XLA Modules:
  0.0 222.5 jit_solution(3460875306081777361)
XLA Ops:
  7.2 0.0 all-reduce.6.cloned.1.call-start
  7.2 0.9 fusion.71
  8.1 4.0 %collective-permute-start.1 = (f32[1,4,1,32,128]{4,3,2,1,0:T(8,128)S(1)}, f32[1,4,1,32,128]{4,3,2,1,0:T(8,128)S(1)}, u32[]{:S(2)}, u32[]{:S(2)}) collective-permute-start(f32[1,4,1,32,128]{4,3,2,1,0:T(8,128)S(1)} %get-tuple-element.39), channel_id=1, source_target_pairs={{0,2},{2,4},{4,6},{6,8},{8,10},{10,12},{12,14},{14,16},{16,18},{18... | collective-permute-start | bytes 196616 | tf_op jit(solution)/shard_map/ppermute | solution.py:15
  12.2 1.4 collective-permute-start
  13.6 6.1 %fusion.61 = (f32[32,32,128]{2,1,0:T(8,128)S(1)}, f32[32,32,128]{2,1,0:T(8,128)S(1)}, f32[32,32,128]{2,1,0:T(8,128)S(1)}, f32[32,32,128]{2,1,0:T(8,128)S(1)}, f3...) fusion(s32[32,32,128]{2,1,0:T(8,128)} %param.14, s32[32,32,128]{2,1,0:T(8,128)} %param.13), kind=kLoop, calls=%fused_computation.183 | loop fusion | flops 1966080 | bytes 4194304 | tf_op jit(solution)/shard_map/mul | solution.py:63
  19.7 0.0 copy-start.4
  19.8 0.0 copy-start.13
  19.8 0.2 constant_dynamic-update-slice_fusion.1
  20.0 0.1 fusion.67
  20.1 1.4 collective-permute-start.2
  21.6 4.0 %collective-permute-start.3 = (f32[1,4,34,1,128]{4,3,2,1,0:T(1,128)S(1)}, f32[1,4,34,1,128]{4,3,2,1,0:T(1,128)S(1)}, u32[]{:S(2)}, u32[]{:S(2)}) collective-permute-start(f32[1,4,34,1,128]{4,3,2,1,0:T(1,128)S(1)} %get-tuple-element.30), channel_id=1, source_target_pairs={{0,1},{2,3},{4,5},{6,7},{8,9},{10,11},{12,13},{14,15},{16,17},{18,... | collective-permute-start | bytes 208904 | tf_op jit(solution)/shard_map/ppermute | solution.py:15
  25.6 0.2 add_sqrt_fusion
  25.8 1.1 collective-permute-done.3
  26.9 2.7 %select_maximum_fusion.12 = f32[1,4,34,34,130]{4,3,2,1,0:T(8,128)S(1)} fusion(f32[1,4,34,1,128]{4,3,2,1,0:T(1,128)S(1)} %collective-permute-done.2, f32[1,4,34,32,128]{4,3,2,1,0:T(8,128)S(1)} %constant_dynamic-update-slice_fusion, f32[1,4,34,1,128]{4,3,2,1,0:T(1,128)S(1)} %collective-permute-done.3), kind=kLoop, calls=%fused_computation.14 | loop fusion | flops 4808960 | bytes 4771968 | tf_op jit(solution)/shard_map/concatenate | solution.py:19
  29.7 8.4 %add_subtract_fusion.3 = (f32[1,4,32,32,128]{4,3,2,1,0:T(8,128)S(1)}, f32[1,4,32,32,128]{4,3,2,1,0:T(8,128)S(1)}) fusion(f32[1,4,32,32,128]{4,3,2,1,0:T(8,128)S(1)} %copy-done.2, f32[1,4,1,32,128]{4,3,2,1,0:T(8,128)S(1)} %collective-permute-done.1, f32[1,4,1,32,128]{4,3,2,1,0:T(8,128)S(1)} %collective-permute-done, ...), kind=kLoop, calls=%fused_computation.140 | loop fusion | flops 22544384 | bytes 32907264 | tf_op jit(solution)/shard_map/sub | solution.py:73
  38.2 2.5 %add_bitcast_fusion.7 = (f32[1,2,1,32,32,128]{5,4,3,1,2,0:T(8,128)S(1)}, f32[1,2,1,32,32,128]{5,4,3,1,2,0:T(8,128)S(1)}) fusion(f32[1,4,32,32,128]{4,3,2,1,0:T(8,128)} %param.9, f32[1,4,32,32,128]{4,3,2,1,0:T(8,128)S(1)} %get-tuple-element.9, f32[1,4,32,32,128]{4,3,2,1,0:T(8,128)S(1)} %get-tuple-element.8, f32[1,4,32,32,128]{4,3,2,1,0:T(8,128)S(1)} %copy-done.2, ...), kind=kLoop, calls=%fused_computation.148 | loop fusion | flops 3407872 | bytes 9961472 | tf_op jit(solution)/shard_map/stack | solution.py:80
  40.8 0.2 pad_maximum_fusion.13
  41.0 0.2 copy.12
  41.2 1.3 collective-permute-start.4
  42.5 4.6 %collective-permute-start.5 = (f32[1,4,1,32,128]{4,3,2,1,0:T(8,128)S(1)}, f32[1,4,1,32,128]{4,3,2,1,0:T(8,128)S(1)}, u32[]{:S(2)}, u32[]{:S(2)}) collective-permute-start(f32[1,4,1,32,128]{4,3,2,1,0:T(8,128)S(1)} %get-tuple-element.37), channel_id=1, source_target_pairs={{0,2},{2,4},{4,6},{6,8},{8,10},{10,12},{12,14},{14,16},{16,18},{18... | collective-permute-start | bytes 196616 | tf_op jit(solution)/shard_map/ppermute | solution.py:15
  47.1 1.3 collective-permute-done.5
  48.4 0.1 pad_maximum_fusion.25
  48.5 1.3 collective-permute-start.6
  49.8 4.2 %collective-permute-start.7 = (f32[1,4,34,1,128]{4,3,2,1,0:T(1,128)S(1)}, f32[1,4,34,1,128]{4,3,2,1,0:T(1,128)S(1)}, u32[]{:S(2)}, u32[]{:S(2)}) collective-permute-start(f32[1,4,34,1,128]{4,3,2,1,0:T(1,128)S(1)} %get-tuple-element.29), channel_id=1, source_target_pairs={{0,1},{2,3},{4,5},{6,7},{8,9},{10,11},{12,13},{14,15},{16,17},{18,... | collective-permute-start | bytes 208904 | tf_op jit(solution)/shard_map/ppermute | solution.py:15
  54.0 1.2 collective-permute-done.7
  55.2 3.6 %select_maximum_fusion.8 = f32[1,4,34,34,130]{4,3,2,1,0:T(8,128)S(1)} fusion(f32[1,4,34,1,128]{4,3,2,1,0:T(1,128)S(1)} %collective-permute-done.6, f32[1,4,34,1,128]{4,3,2,1,0:T(1,128)S(1)} %collective-permute-done.7, f32[1,4,1,32,128]{4,3,2,1,0:T(8,128)S(1)} %collective-permute-done.4, f32[1,4,32,32,128]{4,3,2,1,0:T(8,128)S(1)} %bitcast.25, ...), kind=kLoop, calls=%fused_computation.10 | loop fusion | flops 7213440 | bytes 4771968 | tf_op jit(solution)/shard_map/concatenate | solution.py:19
  58.7 3.0 %pad_maximum_fusion = (f32[1,4,34,33,128]{4,3,2,1,0:T(8,128)}, f32[1,4,34,33,128]{4,3,2,1,0:T(8,128)}) fusion(f32[1,4,34,1,128]{4,3,2,1,0:T(1,128)S(1)} %collective-permute-done.6, f32[1,4,1,32,128]{4,3,2,1,0:T(8,128)S(1)} %collective-permute-done.4, f32[1,4,32,32,128]{4,3,2,1,0:T(8,128)S(1)} %bitcast.26, ...), kind=kLoop, calls=%fused_computation.25 | loop fusion | flops 3446784 | bytes 6963200 | tf_op jit(solution)/shard_map/concatenate | solution.py:19
  61.7 11.2 %add_subtract_fusion.2 = (f32[1,4,32,32,128]{4,3,2,1,0:T(8,128)}, f32[1,4,32,32,128]{4,3,2,1,0:T(8,128)}) fusion(f32[1,4,32,32,128]{4,3,2,1,0:T(8,128)S(1)} %bitcast.27, f32[1,4,1,32,128]{4,3,2,1,0:T(8,128)S(1)} %collective-permute-done.5, f32[1,4,1,32,128]{4,3,2,1,0:T(8,128)S(1)} %collective-permute-done.4, f32[1,4,34,33,128]{4,3,2,1,0:T(8,128)} %get-tuple-element.27, ...), kind=kLoop, calls=%fused_computation.139 | loop fusion | flops 17301504 | bytes 43122688 | tf_op jit(solution)/shard_map/sub | solution.py:73
  72.9 3.0 %add_bitcast_fusion.5 = (f32[1,2,1,32,32,128]{5,4,3,1,2,0:T(8,128)S(1)}, f32[1,2,1,32,32,128]{5,4,3,1,2,0:T(8,128)S(1)}) fusion(f32[1,4,32,32,128]{4,3,2,1,0:T(8,128)} %get-tuple-element.7, f32[1,4,32,32,128]{4,3,2,1,0:T(8,128)} %get-tuple-element.6, f32[1,4,32,32,128]{4,3,2,1,0:T(8,128)S(1)} %bitcast.28, f32[1,4,32,32,128]{4,3,2,1,0:T(8,128)S(1)} %copy-done.2, ...), kind=kLoop, calls=%fused_computation.146 | loop fusion | flops 3407872 | bytes 9961472 | tf_op jit(solution)/shard_map/stack | solution.py:80
  75.9 0.2 pad_maximum_fusion.14
  76.1 0.2 copy.13
  76.3 1.3 collective-permute-start.8
  77.6 4.3 %collective-permute-start.9 = (f32[1,4,1,32,128]{4,3,2,1,0:T(8,128)S(1)}, f32[1,4,1,32,128]{4,3,2,1,0:T(8,128)S(1)}, u32[]{:S(2)}, u32[]{:S(2)}) collective-permute-start(f32[1,4,1,32,128]{4,3,2,1,0:T(8,128)S(1)} %get-tuple-element.35), channel_id=1, source_target_pairs={{0,2},{2,4},{4,6},{6,8},{8,10},{10,12},{12,14},{14,16},{16,18},{18... | collective-permute-start | bytes 196616 | tf_op jit(solution)/shard_map/ppermute | solution.py:15
  81.9 1.3 collective-permute-done.9
  83.2 0.1 pad_maximum_fusion.22
  83.3 1.3 collective-permute-start.10
  84.6 4.0 %collective-permute-start.11 = (f32[1,4,34,1,128]{4,3,2,1,0:T(1,128)S(1)}, f32[1,4,34,1,128]{4,3,2,1,0:T(1,128)S(1)}, u32[]{:S(2)}, u32[]{:S(2)}) collective-permute-start(f32[1,4,34,1,128]{4,3,2,1,0:T(1,128)S(1)} %get-tuple-element.25), channel_id=1, source_target_pairs={{0,1},{2,3},{4,5},{6,7},{8,9},{10,11},{12,13},{14,15},{16,17},{18,... | collective-permute-start | bytes 208904 | tf_op jit(solution)/shard_map/ppermute | solution.py:15
  88.6 1.3 collective-permute-done.11
  89.9 3.6 %select_maximum_fusion.4 = f32[1,4,34,34,130]{4,3,2,1,0:T(8,128)S(1)} fusion(f32[1,4,34,1,128]{4,3,2,1,0:T(1,128)S(1)} %collective-permute-done.10, f32[1,4,34,1,128]{4,3,2,1,0:T(1,128)S(1)} %collective-permute-done.11, f32[1,4,1,32,128]{4,3,2,1,0:T(8,128)S(1)} %collective-permute-done.8, f32[1,4,32,32,128]{4,3,2,1,0:T(8,128)S(1)} %bitcast.33, ...), kind=kLoop, calls=%fused_computation.6 | loop fusion | flops 7213440 | bytes 4771968 | tf_op jit(solution)/shard_map/concatenate | solution.py:19
  93.5 3.0 %pad_maximum_fusion.1 = (f32[1,4,34,33,128]{4,3,2,1,0:T(8,128)}, f32[1,4,34,33,128]{4,3,2,1,0:T(8,128)}) fusion(f32[1,4,34,1,128]{4,3,2,1,0:T(1,128)S(1)} %collective-permute-done.10, f32[1,4,1,32,128]{4,3,2,1,0:T(8,128)S(1)} %collective-permute-done.8, f32[1,4,32,32,128]{4,3,2,1,0:T(8,128)S(1)} %bitcast.34, ...), kind=kLoop, calls=%fused_computation.27 | loop fusion | flops 3446784 | bytes 6963200 | tf_op jit(solution)/shard_map/concatenate | solution.py:19
  96.5 11.2 %add_subtract_fusion.1 = (f32[1,4,32,32,128]{4,3,2,1,0:T(8,128)}, f32[1,4,32,32,128]{4,3,2,1,0:T(8,128)}) fusion(f32[1,4,32,32,128]{4,3,2,1,0:T(8,128)S(1)} %bitcast.35, f32[1,4,1,32,128]{4,3,2,1,0:T(8,128)S(1)} %collective-permute-done.9, f32[1,4,1,32,128]{4,3,2,1,0:T(8,128)S(1)} %collective-permute-done.8, f32[1,4,34,33,128]{4,3,2,1,0:T(8,128)} %get-tuple-element.23, ...), kind=kLoop, calls=%fused_computation.138 | loop fusion | flops 17301504 | bytes 43122688 | tf_op jit(solution)/shard_map/sub | solution.py:73
  107.7 3.0 %add_bitcast_fusion.3 = (f32[1,2,1,32,32,128]{5,4,3,1,2,0:T(8,128)S(1)}, f32[1,2,1,32,32,128]{5,4,3,1,2,0:T(8,128)S(1)}) fusion(f32[1,4,32,32,128]{4,3,2,1,0:T(8,128)} %get-tuple-element.5, f32[1,4,32,32,128]{4,3,2,1,0:T(8,128)} %get-tuple-element.4, f32[1,4,32,32,128]{4,3,2,1,0:T(8,128)S(1)} %bitcast.36, f32[1,4,32,32,128]{4,3,2,1,0:T(8,128)S(1)} %bitcast.29, ...), kind=kLoop, calls=%fused_computation.144 | loop fusion | flops 3407872 | bytes 9961472 | tf_op jit(solution)/shard_map/stack | solution.py:80
  110.7 0.2 pad_maximum_fusion.15
  110.9 0.2 copy.14
  111.1 1.3 collective-permute-start.12
  112.4 4.5 %collective-permute-start.13 = (f32[1,4,1,32,128]{4,3,2,1,0:T(8,128)S(1)}, f32[1,4,1,32,128]{4,3,2,1,0:T(8,128)S(1)}, u32[]{:S(2)}, u32[]{:S(2)}) collective-permute-start(f32[1,4,1,32,128]{4,3,2,1,0:T(8,128)S(1)} %get-tuple-element.33), channel_id=1, source_target_pairs={{0,2},{2,4},{4,6},{6,8},{8,10},{10,12},{12,14},{14,16},{16,18},{18... | collective-permute-start | bytes 196616 | tf_op jit(solution)/shard_map/ppermute | solution.py:15
  117.0 1.3 collective-permute-done.13
  118.3 0.1 pad_maximum_fusion.19
  118.4 1.3 collective-permute-start.14
  119.7 4.0 %collective-permute-start.15 = (f32[1,4,34,1,128]{4,3,2,1,0:T(1,128)S(1)}, f32[1,4,34,1,128]{4,3,2,1,0:T(1,128)S(1)}, u32[]{:S(2)}, u32[]{:S(2)}) collective-permute-start(f32[1,4,34,1,128]{4,3,2,1,0:T(1,128)S(1)} %get-tuple-element.21), channel_id=1, source_target_pairs={{0,1},{2,3},{4,5},{6,7},{8,9},{10,11},{12,13},{14,15},{16,17},{18,... | collective-permute-start | bytes 208904 | tf_op jit(solution)/shard_map/ppermute | solution.py:15
  124.3 0.7 collective-permute-done.15
  125.0 3.6 %select_maximum_fusion = f32[1,4,34,34,130]{4,3,2,1,0:T(8,128)S(1)} fusion(f32[1,4,34,1,128]{4,3,2,1,0:T(1,128)S(1)} %collective-permute-done.14, f32[1,4,34,1,128]{4,3,2,1,0:T(1,128)S(1)} %collective-permute-done.15, f32[1,4,1,32,128]{4,3,2,1,0:T(8,128)S(1)} %collective-permute-done.12, f32[1,4,32,32,128]{4,3,2,1,0:T(8,128)S(1)} %bitcast.41, ...), kind=kLoop, calls=%fused_computation.2 | loop fusion | flops 7213440 | bytes 4771968 | tf_op jit(solution)/shard_map/concatenate | solution.py:19
  128.6 3.0 %pad_maximum_fusion.2 = (f32[1,4,34,33,128]{4,3,2,1,0:T(8,128)}, f32[1,4,34,33,128]{4,3,2,1,0:T(8,128)}) fusion(f32[1,4,34,1,128]{4,3,2,1,0:T(1,128)S(1)} %collective-permute-done.14, f32[1,4,1,32,128]{4,3,2,1,0:T(8,128)S(1)} %collective-permute-done.12, f32[1,4,32,32,128]{4,3,2,1,0:T(8,128)S(1)} %bitcast.42, ...), kind=kLoop, calls=%fused_computation.29 | loop fusion | flops 3446784 | bytes 6963200 | tf_op jit(solution)/shard_map/concatenate | solution.py:19
  131.6 13.1 %add_subtract_fusion = (f32[1,4,32,32,128]{4,3,2,1,0:T(8,128)}, f32[1,4,32,32,128]{4,3,2,1,0:T(8,128)}) fusion(f32[1,4,32,32,128]{4,3,2,1,0:T(8,128)} %bitcast.43, f32[1,4,1,32,128]{4,3,2,1,0:T(8,128)S(1)} %collective-permute-done.13, f32[1,4,1,32,128]{4,3,2,1,0:T(8,128)S(1)} %collective-permute-done.12, f32[1,4,34,33,128]{4,3,2,1,0:T(8,128)} %get-tuple-element.19, ...), kind=kLoop, calls=%fused_computation.137 | loop fusion | flops 17301504 | bytes 43122688 | tf_op jit(solution)/shard_map/sub | solution.py:73
  144.7 3.6 %add_bitcast_fusion.1 = (f32[1,2,1,32,32,128]{5,4,3,1,2,0:T(8,128)S(1)}, f32[1,2,1,32,32,128]{5,4,3,1,2,0:T(8,128)S(1)}) fusion(f32[1,4,32,32,128]{4,3,2,1,0:T(8,128)} %bitcast.44, f32[1,4,32,32,128]{4,3,2,1,0:T(8,128)} %get-tuple-element.3, f32[1,4,32,32,128]{4,3,2,1,0:T(8,128)} %get-tuple-element.2, f32[1,4,32,32,128]{4,3,2,1,0:T(8,128)S(1)} %bitcast.37, ...), kind=kLoop, calls=%fused_computation.142 | loop fusion | flops 3407872 | bytes 9961472 | tf_op jit(solution)/shard_map/stack | solution.py:80
  148.3 0.2 pad_maximum_fusion.16
  148.5 0.2 copy.15
  148.6 0.0 copy-start.12
  148.7 1.3 copy-done.12
  150.0 0.8 copy-done.1
  150.8 1.3 fusion.55
  152.1 0.0 all-reduce.6.cloned.1.call-update
  152.1 61.6 %all-reduce.6.cloned.1.call-done = f32[32,32,128]{2,1,0:T(8,128)} async-done(((f32[32,32,128]{2,1,0:T(8,128)}), f32[32,32,128]{2,1,0:T(8,128)}) %all-reduce.6.cloned.1.call-update) | async-done | bytes 524304 | tf_op jit(solution)/shard_map/psum | solution.py:97
  213.7 1.9 broadcast_multiply_fusion
  (39 shorter events, 0.1 us)
Async XLA Ops:
  7.2 206.6 %all-reduce.6.cloned.1.call-start = ((), (), s32[]{:S(2)}) async-start(), calls=%async_computation | async-start | bytes 1048576 | tf_op jit(solution)/shard_map/psum | solution.py:97
  8.1 11.6 %collective-permute-start.1 = (f32[1,4,1,32,128]{4,3,2,1,0:T(8,128)S(1)}, f32[1,4,1,32,128]{4,3,2,1,0:T(8,128)S(1)}, u32[]{:S(2)}, u32[]{:S(2)}) collective-permute-start(f32[1,4,1,32,128]{4,3,2,1,0:T(8,128)S(1)} %get-tuple-element.39), channel_id=1, source_target_pairs={{0,2},{2,4},{4,6},{6,8},{8,10},{10,12},{12,14},{14,16},{16,18},{18... | collective-permute-start | bytes 196616 | tf_op jit(solution)/shard_map/ppermute | solution.py:15
  12.1 7.6 %copy-start.2 = (f32[1,4,32,32,128]{4,3,2,1,0:T(8,128)S(1)}, f32[1,4,32,32,128]{4,3,2,1,0:T(8,128)}, u32[]{:S(2)}) copy-start(f32[1,4,32,32,128]{4,3,2,1,0:T(8,128)} %param.8) | copy-start | bytes 6291460
  12.2 7.9 %collective-permute-start = (f32[1,4,1,32,128]{4,3,2,1,0:T(8,128)S(1)}, f32[1,4,1,32,128]{4,3,2,1,0:T(8,128)S(1)}, u32[]{:S(2)}, u32[]{:S(2)}) collective-permute-start(f32[1,4,1,32,128]{4,3,2,1,0:T(8,128)S(1)} %get-tuple-element.38), channel_id=1, source_target_pairs={{2,0},{4,2},{6,4},{8,6},{10,8},{12,10},{14,12},{16,14},{18,16},{20... | collective-permute-start | bytes 196616 | tf_op jit(solution)/shard_map/ppermute | solution.py:18
  19.7 10.0 %copy-start.3 = (f32[32,32,128]{2,1,0:T(8,128)}, f32[32,32,128]{2,1,0:T(8,128)S(1)}, u32[]{:S(2)}) copy-start(f32[32,32,128]{2,1,0:T(8,128)S(1)} %get-tuple-element.40) | copy-start | bytes 1572868
  19.7 10.0 %copy-start.4 = (f32[32,32,128]{2,1,0:T(8,128)}, f32[32,32,128]{2,1,0:T(8,128)S(1)}, u32[]{:S(2)}) copy-start(f32[32,32,128]{2,1,0:T(8,128)S(1)} %get-tuple-element.41) | copy-start | bytes 1572868
  19.7 10.0 %copy-start.5 = (f32[32,32,128]{2,1,0:T(8,128)}, f32[32,32,128]{2,1,0:T(8,128)S(1)}, u32[]{:S(2)}) copy-start(f32[32,32,128]{2,1,0:T(8,128)S(1)} %get-tuple-element.42) | copy-start | bytes 1572868
  19.7 10.0 %copy-start.6 = (f32[32,32,128]{2,1,0:T(8,128)}, f32[32,32,128]{2,1,0:T(8,128)S(1)}, u32[]{:S(2)}) copy-start(f32[32,32,128]{2,1,0:T(8,128)S(1)} %get-tuple-element.43) | copy-start | bytes 1572868
  19.7 10.0 %copy-start.7 = (f32[32,32,128]{2,1,0:T(8,128)}, f32[32,32,128]{2,1,0:T(8,128)S(1)}, u32[]{:S(2)}) copy-start(f32[32,32,128]{2,1,0:T(8,128)S(1)} %get-tuple-element.44) | copy-start | bytes 1572868
  19.7 10.0 %copy-start.8 = (f32[32,32,128]{2,1,0:T(8,128)}, f32[32,32,128]{2,1,0:T(8,128)S(1)}, u32[]{:S(2)}) copy-start(f32[32,32,128]{2,1,0:T(8,128)S(1)} %get-tuple-element.45) | copy-start | bytes 1572868
  19.8 5.8 %copy-start.13 = (f32[32,32,128]{2,1,0:T(8,128)S(1)}, f32[32,32,128]{2,1,0:T(8,128)}, u32[]{:S(2)}) copy-start(f32[32,32,128]{2,1,0:T(8,128)} %param.12) | copy-start | bytes 1572868
  19.8 5.8 %copy-start.14 = (f32[32,32,128]{2,1,0:T(8,128)S(1)}, f32[32,32,128]{2,1,0:T(8,128)}, u32[]{:S(2)}) copy-start(f32[32,32,128]{2,1,0:T(8,128)} %param.11) | copy-start | bytes 1572868
  20.1 5.7 %collective-permute-start.2 = (f32[1,4,34,1,128]{4,3,2,1,0:T(1,128)S(1)}, f32[1,4,34,1,128]{4,3,2,1,0:T(1,128)S(1)}, u32[]{:S(2)}, u32[]{:S(2)}) collective-permute-start(f32[1,4,34,1,128]{4,3,2,1,0:T(1,128)S(1)} %get-tuple-element.31), channel_id=1, source_target_pairs={{1,0},{3,2},{5,4},{7,6},{9,8},{11,10},{13,12},{15,14},{17,16},{19,... | collective-permute-start | bytes 208904 | tf_op jit(solution)/shard_map/ppermute | solution.py:18
  21.6 5.3 %collective-permute-start.3 = (f32[1,4,34,1,128]{4,3,2,1,0:T(1,128)S(1)}, f32[1,4,34,1,128]{4,3,2,1,0:T(1,128)S(1)}, u32[]{:S(2)}, u32[]{:S(2)}) collective-permute-start(f32[1,4,34,1,128]{4,3,2,1,0:T(1,128)S(1)} %get-tuple-element.30), channel_id=1, source_target_pairs={{0,1},{2,3},{4,5},{6,7},{8,9},{10,11},{12,13},{14,15},{16,17},{18,... | collective-permute-start | bytes 208904 | tf_op jit(solution)/shard_map/ppermute | solution.py:15
  25.8 12.4 %copy-start.9 = (f32[32,32,128]{2,1,0:T(8,128)}, f32[32,32,128]{2,1,0:T(8,128)S(1)}, u32[]{:S(2)}) copy-start(f32[32,32,128]{2,1,0:T(8,128)S(1)} %get-tuple-element.46) | copy-start | bytes 1572868
  25.8 12.4 %copy-start.10 = (f32[32,32,128]{2,1,0:T(8,128)}, f32[32,32,128]{2,1,0:T(8,128)S(1)}, u32[]{:S(2)}) copy-start(f32[32,32,128]{2,1,0:T(8,128)S(1)} %get-tuple-element.47) | copy-start | bytes 1572868
  29.7 8.5 %copy-start.11 = (f32[32,32,128]{2,1,0:T(8,128)S(1)}, f32[32,32,128]{2,1,0:T(8,128)}, u32[]{:S(2)}) copy-start(f32[32,32,128]{2,1,0:T(8,128)} %param.10) | copy-start | bytes 1572868
  41.2 5.9 %collective-permute-start.4 = (f32[1,4,1,32,128]{4,3,2,1,0:T(8,128)S(1)}, f32[1,4,1,32,128]{4,3,2,1,0:T(8,128)S(1)}, u32[]{:S(2)}, u32[]{:S(2)}) collective-permute-start(f32[1,4,1,32,128]{4,3,2,1,0:T(8,128)S(1)} %get-tuple-element.36), channel_id=1, source_target_pairs={{2,0},{4,2},{6,4},{8,6},{10,8},{12,10},{14,12},{16,14},{18,16},{20... | collective-permute-start | bytes 196616 | tf_op jit(solution)/shard_map/ppermute | solution.py:18
  42.5 5.9 %collective-permute-start.5 = (f32[1,4,1,32,128]{4,3,2,1,0:T(8,128)S(1)}, f32[1,4,1,32,128]{4,3,2,1,0:T(8,128)S(1)}, u32[]{:S(2)}, u32[]{:S(2)}) collective-permute-start(f32[1,4,1,32,128]{4,3,2,1,0:T(8,128)S(1)} %get-tuple-element.37), channel_id=1, source_target_pairs={{0,2},{2,4},{4,6},{6,8},{8,10},{10,12},{12,14},{14,16},{16,18},{18... | collective-permute-start | bytes 196616 | tf_op jit(solution)/shard_map/ppermute | solution.py:15
  48.5 5.5 %collective-permute-start.6 = (f32[1,4,34,1,128]{4,3,2,1,0:T(1,128)S(1)}, f32[1,4,34,1,128]{4,3,2,1,0:T(1,128)S(1)}, u32[]{:S(2)}, u32[]{:S(2)}) collective-permute-start(f32[1,4,34,1,128]{4,3,2,1,0:T(1,128)S(1)} %get-tuple-element.28), channel_id=1, source_target_pairs={{1,0},{3,2},{5,4},{7,6},{9,8},{11,10},{13,12},{15,14},{17,16},{19,... | collective-permute-start | bytes 208904 | tf_op jit(solution)/shard_map/ppermute | solution.py:18
  49.8 5.3 %collective-permute-start.7 = (f32[1,4,34,1,128]{4,3,2,1,0:T(1,128)S(1)}, f32[1,4,34,1,128]{4,3,2,1,0:T(1,128)S(1)}, u32[]{:S(2)}, u32[]{:S(2)}) collective-permute-start(f32[1,4,34,1,128]{4,3,2,1,0:T(1,128)S(1)} %get-tuple-element.29), channel_id=1, source_target_pairs={{0,1},{2,3},{4,5},{6,7},{8,9},{10,11},{12,13},{14,15},{16,17},{18,... | collective-permute-start | bytes 208904 | tf_op jit(solution)/shard_map/ppermute | solution.py:15
  76.3 5.6 %collective-permute-start.8 = (f32[1,4,1,32,128]{4,3,2,1,0:T(8,128)S(1)}, f32[1,4,1,32,128]{4,3,2,1,0:T(8,128)S(1)}, u32[]{:S(2)}, u32[]{:S(2)}) collective-permute-start(f32[1,4,1,32,128]{4,3,2,1,0:T(8,128)S(1)} %get-tuple-element.34), channel_id=1, source_target_pairs={{2,0},{4,2},{6,4},{8,6},{10,8},{12,10},{14,12},{16,14},{18,16},{20... | collective-permute-start | bytes 196616 | tf_op jit(solution)/shard_map/ppermute | solution.py:18
  77.6 5.6 %collective-permute-start.9 = (f32[1,4,1,32,128]{4,3,2,1,0:T(8,128)S(1)}, f32[1,4,1,32,128]{4,3,2,1,0:T(8,128)S(1)}, u32[]{:S(2)}, u32[]{:S(2)}) collective-permute-start(f32[1,4,1,32,128]{4,3,2,1,0:T(8,128)S(1)} %get-tuple-element.35), channel_id=1, source_target_pairs={{0,2},{2,4},{4,6},{6,8},{8,10},{10,12},{12,14},{14,16},{16,18},{18... | collective-permute-start | bytes 196616 | tf_op jit(solution)/shard_map/ppermute | solution.py:15
  83.3 5.3 %collective-permute-start.10 = (f32[1,4,34,1,128]{4,3,2,1,0:T(1,128)S(1)}, f32[1,4,34,1,128]{4,3,2,1,0:T(1,128)S(1)}, u32[]{:S(2)}, u32[]{:S(2)}) collective-permute-start(f32[1,4,34,1,128]{4,3,2,1,0:T(1,128)S(1)} %get-tuple-element.24), channel_id=1, source_target_pairs={{1,0},{3,2},{5,4},{7,6},{9,8},{11,10},{13,12},{15,14},{17,16},{19,... | collective-permute-start | bytes 208904 | tf_op jit(solution)/shard_map/ppermute | solution.py:18
  84.6 5.3 %collective-permute-start.11 = (f32[1,4,34,1,128]{4,3,2,1,0:T(1,128)S(1)}, f32[1,4,34,1,128]{4,3,2,1,0:T(1,128)S(1)}, u32[]{:S(2)}, u32[]{:S(2)}) collective-permute-start(f32[1,4,34,1,128]{4,3,2,1,0:T(1,128)S(1)} %get-tuple-element.25), channel_id=1, source_target_pairs={{0,1},{2,3},{4,5},{6,7},{8,9},{10,11},{12,13},{14,15},{16,17},{18,... | collective-permute-start | bytes 208904 | tf_op jit(solution)/shard_map/ppermute | solution.py:15
  111.1 17.5 %copy-start = (f32[1,2,2,32,32,128]{5,4,3,2,1,0:T(8,128)}, f32[1,2,2,32,32,128]{5,4,3,2,1,0:T(8,128)S(1)}, u32[]{:S(2)}) copy-start(f32[1,2,2,32,32,128]{5,4,3,2,1,0:T(8,128)S(1)} %copy.14) | copy-start | bytes 6291460
  111.1 5.9 %collective-permute-start.12 = (f32[1,4,1,32,128]{4,3,2,1,0:T(8,128)S(1)}, f32[1,4,1,32,128]{4,3,2,1,0:T(8,128)S(1)}, u32[]{:S(2)}, u32[]{:S(2)}) collective-permute-start(f32[1,4,1,32,128]{4,3,2,1,0:T(8,128)S(1)} %get-tuple-element.32), channel_id=1, source_target_pairs={{2,0},{4,2},{6,4},{8,6},{10,8},{12,10},{14,12},{16,14},{18,16},{20... | collective-permute-start | bytes 196616 | tf_op jit(solution)/shard_map/ppermute | solution.py:18
  112.4 5.9 %collective-permute-start.13 = (f32[1,4,1,32,128]{4,3,2,1,0:T(8,128)S(1)}, f32[1,4,1,32,128]{4,3,2,1,0:T(8,128)S(1)}, u32[]{:S(2)}, u32[]{:S(2)}) collective-permute-start(f32[1,4,1,32,128]{4,3,2,1,0:T(8,128)S(1)} %get-tuple-element.33), channel_id=1, source_target_pairs={{0,2},{2,4},{4,6},{6,8},{8,10},{10,12},{12,14},{14,16},{16,18},{18... | collective-permute-start | bytes 196616 | tf_op jit(solution)/shard_map/ppermute | solution.py:15
  118.4 5.9 %collective-permute-start.14 = (f32[1,4,34,1,128]{4,3,2,1,0:T(1,128)S(1)}, f32[1,4,34,1,128]{4,3,2,1,0:T(1,128)S(1)}, u32[]{:S(2)}, u32[]{:S(2)}) collective-permute-start(f32[1,4,34,1,128]{4,3,2,1,0:T(1,128)S(1)} %get-tuple-element.20), channel_id=1, source_target_pairs={{1,0},{3,2},{5,4},{7,6},{9,8},{11,10},{13,12},{15,14},{17,16},{19,... | collective-permute-start | bytes 208904 | tf_op jit(solution)/shard_map/ppermute | solution.py:18
  119.7 5.3 %collective-permute-start.15 = (f32[1,4,34,1,128]{4,3,2,1,0:T(1,128)S(1)}, f32[1,4,34,1,128]{4,3,2,1,0:T(1,128)S(1)}, u32[]{:S(2)}, u32[]{:S(2)}) collective-permute-start(f32[1,4,34,1,128]{4,3,2,1,0:T(1,128)S(1)} %get-tuple-element.21), channel_id=1, source_target_pairs={{0,1},{2,3},{4,5},{6,7},{8,9},{10,11},{12,13},{14,15},{16,17},{18,... | collective-permute-start | bytes 208904 | tf_op jit(solution)/shard_map/ppermute | solution.py:15
  148.5 2.3 %copy-start.1 = (f32[1,2,2,32,32,128]{5,4,3,2,1,0:T(8,128)S(1)}, f32[1,2,2,32,32,128]{5,4,3,2,1,0:T(8,128)}, u32[]{:S(2)}) copy-start(f32[1,2,2,32,32,128]{5,4,3,2,1,0:T(8,128)} %copy-done) | copy-start | bytes 6291460
  148.6 1.3 copy-start.12
Sparse Core Ops, SparseCore 0:
  152.2 61.4 all-reduce.5
where the time goes:
time: 223 us; the launch traced here: 222 us
  other arithmetic  88.9 us (40%)
  waiting for transfers between devices  69.8 us (31%)
  starting transfers between devices  44.3 us (20%)
  between operations  15.3 us (7%)
  local copies, waits for them, and re-layouts  4.16 us (2%)
    psum x1, waiting for transfers between devices, local(): image = lax.psum(covered * correlation, 'shot') / ITERS  61.6 us
    sub x4, other arithmetic, advance(): across = second_x + second_y + second_z - along  44 us
    ppermute x8, starting transfers between devices, extended(): lax.ppermute(lax.slice_in_dim(block, block.shape[dim] - width, None, axis...  33.6 us
    concatenate x7, other arithmetic, extended(): block = jnp.concatenate([low, block, high], axis=dim)  22.4 us
    another operation x8, other arithmetic, advance(): return jnp.stack([next_p, next_q], axis=2).reshape(centre.shape)  12.8 us
    ppermute x8, starting transfers between devices, extended(): lax.ppermute(lax.slice_in_dim(block, 0, width, axis=dim), axis, backward)  10.6 us
    ppermute x8, waiting for transfers between devices, extended(): lax.ppermute(lax.slice_in_dim(block, block.shape[dim] - width, None, axis...  8.18 us
    mul x1, other arithmetic, advance(): normal_x * normal_x * second_x + normal_y * normal_y * second_y  6.06 us
  transfers between devices with their start and end apart: 17, of which 8 were waited for; matrix products, arithmetic and copies ran while one was open for 3% of the time, Pallas kernels for 0%

commit v1 on v0

--- a/solution.py
+++ b/solution.py
@@ -94,7 +94,7 @@
         correlation = correlation + fresh[0, 0] * fresh[0, 2]
         previous, current = (current, fresh)
     covered = aperture[0, 0, 0].astype(jnp.float32)
-    image = lax.psum(covered * correlation, "shot") / ITERS
+    image = jnp.sum(lax.all_gather(covered * correlation, "shot"), axis=0) / ITERS
     return (current, image)
 
 

time: 223 us -> 209 us (0.937)
  waiting for transfers between devices: 69.8 us -> 54.4 us
    psum x1 -> x0, waiting for transfers between devices: 61.6 us -> none  [local(): image = lax.psum(covered * correlation, 'shot') / ITERS]
    all_gather x0 -> x1, waiting for transfers between devices: none -> 46.2 us  [local(): lax.all_gather(covered * correlation, 'shot')]
where the time goes in v1:
time: 209 us; the launch traced here: 208 us
  other arithmetic  89.7 us (43%)
  waiting for transfers between devices  54.4 us (26%)
  starting transfers between devices  44.3 us (21%)
  between operations  15.3 us (7%)
  local copies, waits for them, and re-layouts  4.16 us (2%)
    all_gather x1, waiting for transfers between devices, local(): lax.all_gather(covered * correlation, 'shot')  46.2 us
    sub x4, other arithmetic, advance(): across = second_x + second_y + second_z - along  44 us
    ppermute x8, starting transfers between devices, extended(): lax.ppermute(lax.slice_in_dim(block, block.shape[dim] - width, None, axis...  33.6 us
    concatenate x7, other arithmetic, extended(): block = jnp.concatenate([low, block, high], axis=dim)  22.4 us
    another operation x8, other arithmetic, advance(): return jnp.stack([next_p, next_q], axis=2).reshape(centre.shape)  12.8 us
    ppermute x8, starting transfers between devices, extended(): lax.ppermute(lax.slice_in_dim(block, 0, width, axis=dim), axis, backward)  10.6 us
    ppermute x8, waiting for transfers between devices, extended(): lax.ppermute(lax.slice_in_dim(block, block.shape[dim] - width, None, axis...  8.18 us
    mul x1, other arithmetic, advance(): normal_x * normal_x * second_x + normal_y * normal_y * second_y  6.06 us
  transfers between devices with their start and end apart: 17, of which 8 were waited for; matrix products, arithmetic and copies ran while one was open for 3% of the time, Pallas kernels for 0%

profile of v1, /device:TPU:1, one launch (start us, length us, event | category | flops | bytes accessed | tf_op | source)
XLA Modules:
  0.0 207.9 jit_solution(9468310593393684555)
XLA Ops:
  7.2 0.0 all-gather.3.cloned.1.call-start
  7.2 0.9 fusion.70
  8.1 4.0 %collective-permute-start.1 = (f32[1,4,1,32,128]{4,3,2,1,0:T(8,128)S(1)}, f32[1,4,1,32,128]{4,3,2,1,0:T(8,128)S(1)}, u32[]{:S(2)}, u32[]{:S(2)}) collective-permute-start(f32[1,4,1,32,128]{4,3,2,1,0:T(8,128)S(1)} %get-tuple-element.39), channel_id=1, source_target_pairs={{0,2},{2,4},{4,6},{6,8},{8,10},{10,12},{12,14},{14,16},{16,18},{18... | collective-permute-start | bytes 196616 | tf_op jit(solution)/shard_map/ppermute | solution.py:15
  12.2 1.4 collective-permute-start
  13.6 6.1 %fusion.60 = (f32[32,32,128]{2,1,0:T(8,128)S(1)}, f32[32,32,128]{2,1,0:T(8,128)S(1)}, f32[32,32,128]{2,1,0:T(8,128)S(1)}, f32[32,32,128]{2,1,0:T(8,128)S(1)}, f3...) fusion(s32[32,32,128]{2,1,0:T(8,128)} %param.14, s32[32,32,128]{2,1,0:T(8,128)} %param.13), kind=kLoop, calls=%fused_computation.182 | loop fusion | flops 1966080 | bytes 4194304 | tf_op jit(solution)/shard_map/mul | solution.py:63
  19.7 0.0 copy-start.4
  19.8 0.0 copy-start.13
  19.8 0.2 constant_dynamic-update-slice_fusion.1
  20.0 0.1 fusion.66
  20.1 1.4 collective-permute-start.2
  21.6 4.0 %collective-permute-start.3 = (f32[1,4,34,1,128]{4,3,2,1,0:T(1,128)S(1)}, f32[1,4,34,1,128]{4,3,2,1,0:T(1,128)S(1)}, u32[]{:S(2)}, u32[]{:S(2)}) collective-permute-start(f32[1,4,34,1,128]{4,3,2,1,0:T(1,128)S(1)} %get-tuple-element.30), channel_id=1, source_target_pairs={{0,1},{2,3},{4,5},{6,7},{8,9},{10,11},{12,13},{14,15},{16,17},{18,... | collective-permute-start | bytes 208904 | tf_op jit(solution)/shard_map/ppermute | solution.py:15
  25.6 0.2 add_sqrt_fusion
  25.8 1.1 collective-permute-done.3
  26.9 2.7 %select_maximum_fusion.12 = f32[1,4,34,34,130]{4,3,2,1,0:T(8,128)S(1)} fusion(f32[1,4,34,1,128]{4,3,2,1,0:T(1,128)S(1)} %collective-permute-done.2, f32[1,4,34,32,128]{4,3,2,1,0:T(8,128)S(1)} %constant_dynamic-update-slice_fusion, f32[1,4,34,1,128]{4,3,2,1,0:T(1,128)S(1)} %collective-permute-done.3), kind=kLoop, calls=%fused_computation.14 | loop fusion | flops 4808960 | bytes 4771968 | tf_op jit(solution)/shard_map/concatenate | solution.py:19
  29.7 8.4 %add_subtract_fusion.3 = (f32[1,4,32,32,128]{4,3,2,1,0:T(8,128)S(1)}, f32[1,4,32,32,128]{4,3,2,1,0:T(8,128)S(1)}) fusion(f32[1,4,32,32,128]{4,3,2,1,0:T(8,128)S(1)} %copy-done.2, f32[1,4,1,32,128]{4,3,2,1,0:T(8,128)S(1)} %collective-permute-done.1, f32[1,4,1,32,128]{4,3,2,1,0:T(8,128)S(1)} %collective-permute-done, ...), kind=kLoop, calls=%fused_computation.140 | loop fusion | flops 22544384 | bytes 32907264 | tf_op jit(solution)/shard_map/sub | solution.py:73
  38.2 2.5 %add_bitcast_fusion.7 = (f32[1,2,1,32,32,128]{5,4,3,1,2,0:T(8,128)S(1)}, f32[1,2,1,32,32,128]{5,4,3,1,2,0:T(8,128)S(1)}) fusion(f32[1,4,32,32,128]{4,3,2,1,0:T(8,128)} %param.9, f32[1,4,32,32,128]{4,3,2,1,0:T(8,128)S(1)} %get-tuple-element.9, f32[1,4,32,32,128]{4,3,2,1,0:T(8,128)S(1)} %get-tuple-element.8, f32[1,4,32,32,128]{4,3,2,1,0:T(8,128)S(1)} %copy-done.2, ...), kind=kLoop, calls=%fused_computation.148 | loop fusion | flops 3407872 | bytes 9961472 | tf_op jit(solution)/shard_map/stack | solution.py:80
  40.8 0.2 pad_maximum_fusion.13
  41.0 0.2 copy.17
  41.2 1.3 collective-permute-start.4
  42.5 4.6 %collective-permute-start.5 = (f32[1,4,1,32,128]{4,3,2,1,0:T(8,128)S(1)}, f32[1,4,1,32,128]{4,3,2,1,0:T(8,128)S(1)}, u32[]{:S(2)}, u32[]{:S(2)}) collective-permute-start(f32[1,4,1,32,128]{4,3,2,1,0:T(8,128)S(1)} %get-tuple-element.37), channel_id=1, source_target_pairs={{0,2},{2,4},{4,6},{6,8},{8,10},{10,12},{12,14},{14,16},{16,18},{18... | collective-permute-start | bytes 196616 | tf_op jit(solution)/shard_map/ppermute | solution.py:15
  47.1 1.3 collective-permute-done.5
  48.4 0.1 pad_maximum_fusion.25
  48.5 1.3 collective-permute-start.6
  49.8 4.2 %collective-permute-start.7 = (f32[1,4,34,1,128]{4,3,2,1,0:T(1,128)S(1)}, f32[1,4,34,1,128]{4,3,2,1,0:T(1,128)S(1)}, u32[]{:S(2)}, u32[]{:S(2)}) collective-permute-start(f32[1,4,34,1,128]{4,3,2,1,0:T(1,128)S(1)} %get-tuple-element.29), channel_id=1, source_target_pairs={{0,1},{2,3},{4,5},{6,7},{8,9},{10,11},{12,13},{14,15},{16,17},{18,... | collective-permute-start | bytes 208904 | tf_op jit(solution)/shard_map/ppermute | solution.py:15
  54.0 1.2 collective-permute-done.7
  55.2 3.6 %select_maximum_fusion.8 = f32[1,4,34,34,130]{4,3,2,1,0:T(8,128)S(1)} fusion(f32[1,4,34,1,128]{4,3,2,1,0:T(1,128)S(1)} %collective-permute-done.6, f32[1,4,34,1,128]{4,3,2,1,0:T(1,128)S(1)} %collective-permute-done.7, f32[1,4,1,32,128]{4,3,2,1,0:T(8,128)S(1)} %collective-permute-done.4, f32[1,4,32,32,128]{4,3,2,1,0:T(8,128)S(1)} %bitcast.23, ...), kind=kLoop, calls=%fused_computation.10 | loop fusion | flops 7213440 | bytes 4771968 | tf_op jit(solution)/shard_map/concatenate | solution.py:19
  58.7 3.0 %pad_maximum_fusion = (f32[1,4,34,33,128]{4,3,2,1,0:T(8,128)}, f32[1,4,34,33,128]{4,3,2,1,0:T(8,128)}) fusion(f32[1,4,34,1,128]{4,3,2,1,0:T(1,128)S(1)} %collective-permute-done.6, f32[1,4,1,32,128]{4,3,2,1,0:T(8,128)S(1)} %collective-permute-done.4, f32[1,4,32,32,128]{4,3,2,1,0:T(8,128)S(1)} %bitcast.24, ...), kind=kLoop, calls=%fused_computation.25 | loop fusion | flops 3446784 | bytes 6963200 | tf_op jit(solution)/shard_map/concatenate | solution.py:19
  61.7 11.2 %add_subtract_fusion.2 = (f32[1,4,32,32,128]{4,3,2,1,0:T(8,128)}, f32[1,4,32,32,128]{4,3,2,1,0:T(8,128)}) fusion(f32[1,4,32,32,128]{4,3,2,1,0:T(8,128)S(1)} %bitcast.25, f32[1,4,1,32,128]{4,3,2,1,0:T(8,128)S(1)} %collective-permute-done.5, f32[1,4,1,32,128]{4,3,2,1,0:T(8,128)S(1)} %collective-permute-done.4, f32[1,4,34,33,128]{4,3,2,1,0:T(8,128)} %get-tuple-element.27, ...), kind=kLoop, calls=%fused_computation.139 | loop fusion | flops 17301504 | bytes 43122688 | tf_op jit(solution)/shard_map/sub | solution.py:73
  72.9 3.0 %add_bitcast_fusion.5 = (f32[1,2,1,32,32,128]{5,4,3,1,2,0:T(8,128)S(1)}, f32[1,2,1,32,32,128]{5,4,3,1,2,0:T(8,128)S(1)}) fusion(f32[1,4,32,32,128]{4,3,2,1,0:T(8,128)} %get-tuple-element.7, f32[1,4,32,32,128]{4,3,2,1,0:T(8,128)} %get-tuple-element.6, f32[1,4,32,32,128]{4,3,2,1,0:T(8,128)S(1)} %bitcast.26, f32[1,4,32,32,128]{4,3,2,1,0:T(8,128)S(1)} %copy-done.2, ...), kind=kLoop, calls=%fused_computation.146 | loop fusion | flops 3407872 | bytes 9961472 | tf_op jit(solution)/shard_map/stack | solution.py:80
  75.9 0.2 pad_maximum_fusion.14
  76.1 0.2 copy.18
  76.3 1.3 collective-permute-start.8
  77.6 4.3 %collective-permute-start.9 = (f32[1,4,1,32,128]{4,3,2,1,0:T(8,128)S(1)}, f32[1,4,1,32,128]{4,3,2,1,0:T(8,128)S(1)}, u32[]{:S(2)}, u32[]{:S(2)}) collective-permute-start(f32[1,4,1,32,128]{4,3,2,1,0:T(8,128)S(1)} %get-tuple-element.35), channel_id=1, source_target_pairs={{0,2},{2,4},{4,6},{6,8},{8,10},{10,12},{12,14},{14,16},{16,18},{18... | collective-permute-start | bytes 196616 | tf_op jit(solution)/shard_map/ppermute | solution.py:15
  81.9 1.3 collective-permute-done.9
  83.2 0.1 pad_maximum_fusion.22
  83.3 1.3 collective-permute-start.10
  84.6 4.0 %collective-permute-start.11 = (f32[1,4,34,1,128]{4,3,2,1,0:T(1,128)S(1)}, f32[1,4,34,1,128]{4,3,2,1,0:T(1,128)S(1)}, u32[]{:S(2)}, u32[]{:S(2)}) collective-permute-start(f32[1,4,34,1,128]{4,3,2,1,0:T(1,128)S(1)} %get-tuple-element.25), channel_id=1, source_target_pairs={{0,1},{2,3},{4,5},{6,7},{8,9},{10,11},{12,13},{14,15},{16,17},{18,... | collective-permute-start | bytes 208904 | tf_op jit(solution)/shard_map/ppermute | solution.py:15
  88.6 1.3 collective-permute-done.11
  89.9 3.6 %select_maximum_fusion.4 = f32[1,4,34,34,130]{4,3,2,1,0:T(8,128)S(1)} fusion(f32[1,4,34,1,128]{4,3,2,1,0:T(1,128)S(1)} %collective-permute-done.10, f32[1,4,34,1,128]{4,3,2,1,0:T(1,128)S(1)} %collective-permute-done.11, f32[1,4,1,32,128]{4,3,2,1,0:T(8,128)S(1)} %collective-permute-done.8, f32[1,4,32,32,128]{4,3,2,1,0:T(8,128)S(1)} %bitcast.31, ...), kind=kLoop, calls=%fused_computation.6 | loop fusion | flops 7213440 | bytes 4771968 | tf_op jit(solution)/shard_map/concatenate | solution.py:19
  93.5 3.0 %pad_maximum_fusion.1 = (f32[1,4,34,33,128]{4,3,2,1,0:T(8,128)}, f32[1,4,34,33,128]{4,3,2,1,0:T(8,128)}) fusion(f32[1,4,34,1,128]{4,3,2,1,0:T(1,128)S(1)} %collective-permute-done.10, f32[1,4,1,32,128]{4,3,2,1,0:T(8,128)S(1)} %collective-permute-done.8, f32[1,4,32,32,128]{4,3,2,1,0:T(8,128)S(1)} %bitcast.32, ...), kind=kLoop, calls=%fused_computation.27 | loop fusion | flops 3446784 | bytes 6963200 | tf_op jit(solution)/shard_map/concatenate | solution.py:19
  96.5 11.2 %add_subtract_fusion.1 = (f32[1,4,32,32,128]{4,3,2,1,0:T(8,128)}, f32[1,4,32,32,128]{4,3,2,1,0:T(8,128)}) fusion(f32[1,4,32,32,128]{4,3,2,1,0:T(8,128)S(1)} %bitcast.33, f32[1,4,1,32,128]{4,3,2,1,0:T(8,128)S(1)} %collective-permute-done.9, f32[1,4,1,32,128]{4,3,2,1,0:T(8,128)S(1)} %collective-permute-done.8, f32[1,4,34,33,128]{4,3,2,1,0:T(8,128)} %get-tuple-element.23, ...), kind=kLoop, calls=%fused_computation.138 | loop fusion | flops 17301504 | bytes 43122688 | tf_op jit(solution)/shard_map/sub | solution.py:73
  107.7 3.0 %add_bitcast_fusion.3 = (f32[1,2,1,32,32,128]{5,4,3,1,2,0:T(8,128)S(1)}, f32[1,2,1,32,32,128]{5,4,3,1,2,0:T(8,128)S(1)}) fusion(f32[1,4,32,32,128]{4,3,2,1,0:T(8,128)} %get-tuple-element.5, f32[1,4,32,32,128]{4,3,2,1,0:T(8,128)} %get-tuple-element.4, f32[1,4,32,32,128]{4,3,2,1,0:T(8,128)S(1)} %bitcast.34, f32[1,4,32,32,128]{4,3,2,1,0:T(8,128)S(1)} %bitcast.27, ...), kind=kLoop, calls=%fused_computation.144 | loop fusion | flops 3407872 | bytes 9961472 | tf_op jit(solution)/shard_map/stack | solution.py:80
  110.7 0.2 pad_maximum_fusion.15
  110.9 0.2 copy.19
  111.1 1.3 collective-permute-start.12
  112.4 4.5 %collective-permute-start.13 = (f32[1,4,1,32,128]{4,3,2,1,0:T(8,128)S(1)}, f32[1,4,1,32,128]{4,3,2,1,0:T(8,128)S(1)}, u32[]{:S(2)}, u32[]{:S(2)}) collective-permute-start(f32[1,4,1,32,128]{4,3,2,1,0:T(8,128)S(1)} %get-tuple-element.33), channel_id=1, source_target_pairs={{0,2},{2,4},{4,6},{6,8},{8,10},{10,12},{12,14},{14,16},{16,18},{18... | collective-permute-start | bytes 196616 | tf_op jit(solution)/shard_map/ppermute | solution.py:15
  117.0 1.3 collective-permute-done.13
  118.3 0.1 pad_maximum_fusion.19
  118.4 1.3 collective-permute-start.14
  119.7 4.0 %collective-permute-start.15 = (f32[1,4,34,1,128]{4,3,2,1,0:T(1,128)S(1)}, f32[1,4,34,1,128]{4,3,2,1,0:T(1,128)S(1)}, u32[]{:S(2)}, u32[]{:S(2)}) collective-permute-start(f32[1,4,34,1,128]{4,3,2,1,0:T(1,128)S(1)} %get-tuple-element.21), channel_id=1, source_target_pairs={{0,1},{2,3},{4,5},{6,7},{8,9},{10,11},{12,13},{14,15},{16,17},{18,... | collective-permute-start | bytes 208904 | tf_op jit(solution)/shard_map/ppermute | solution.py:15
  124.3 0.7 collective-permute-done.15
  125.0 3.6 %select_maximum_fusion = f32[1,4,34,34,130]{4,3,2,1,0:T(8,128)S(1)} fusion(f32[1,4,34,1,128]{4,3,2,1,0:T(1,128)S(1)} %collective-permute-done.14, f32[1,4,34,1,128]{4,3,2,1,0:T(1,128)S(1)} %collective-permute-done.15, f32[1,4,1,32,128]{4,3,2,1,0:T(8,128)S(1)} %collective-permute-done.12, f32[1,4,32,32,128]{4,3,2,1,0:T(8,128)S(1)} %bitcast.39, ...), kind=kLoop, calls=%fused_computation.2 | loop fusion | flops 7213440 | bytes 4771968 | tf_op jit(solution)/shard_map/concatenate | solution.py:19
  128.6 3.0 %pad_maximum_fusion.2 = (f32[1,4,34,33,128]{4,3,2,1,0:T(8,128)}, f32[1,4,34,33,128]{4,3,2,1,0:T(8,128)}) fusion(f32[1,4,34,1,128]{4,3,2,1,0:T(1,128)S(1)} %collective-permute-done.14, f32[1,4,1,32,128]{4,3,2,1,0:T(8,128)S(1)} %collective-permute-done.12, f32[1,4,32,32,128]{4,3,2,1,0:T(8,128)S(1)} %bitcast.40, ...), kind=kLoop, calls=%fused_computation.29 | loop fusion | flops 3446784 | bytes 6963200 | tf_op jit(solution)/shard_map/concatenate | solution.py:19
  131.6 13.1 %add_subtract_fusion = (f32[1,4,32,32,128]{4,3,2,1,0:T(8,128)}, f32[1,4,32,32,128]{4,3,2,1,0:T(8,128)}) fusion(f32[1,4,32,32,128]{4,3,2,1,0:T(8,128)} %bitcast.41, f32[1,4,1,32,128]{4,3,2,1,0:T(8,128)S(1)} %collective-permute-done.13, f32[1,4,1,32,128]{4,3,2,1,0:T(8,128)S(1)} %collective-permute-done.12, f32[1,4,34,33,128]{4,3,2,1,0:T(8,128)} %get-tuple-element.19, ...), kind=kLoop, calls=%fused_computation.137 | loop fusion | flops 17301504 | bytes 43122688 | tf_op jit(solution)/shard_map/sub | solution.py:73
  144.7 3.6 %add_bitcast_fusion.1 = (f32[1,2,1,32,32,128]{5,4,3,1,2,0:T(8,128)S(1)}, f32[1,2,1,32,32,128]{5,4,3,1,2,0:T(8,128)S(1)}) fusion(f32[1,4,32,32,128]{4,3,2,1,0:T(8,128)} %bitcast.42, f32[1,4,32,32,128]{4,3,2,1,0:T(8,128)} %get-tuple-element.3, f32[1,4,32,32,128]{4,3,2,1,0:T(8,128)} %get-tuple-element.2, f32[1,4,32,32,128]{4,3,2,1,0:T(8,128)S(1)} %bitcast.35, ...), kind=kLoop, calls=%fused_computation.142 | loop fusion | flops 3407872 | bytes 9961472 | tf_op jit(solution)/shard_map/stack | solution.py:80
  148.3 0.2 pad_maximum_fusion.16
  148.5 0.2 copy.20
  148.7 1.3 copy-done.12
  150.0 0.8 copy-done.1
  150.8 1.3 fusion.54
  152.1 0.0 all-gather.3.cloned.1.call-update
  152.1 46.2 %all-gather.3.cloned.1.call-done = f32[4,1,32,32,128]{4,3,2,1,0:T(8,128)} async-done(((f32[1,1,32,32,128]{4,3,2,1,0:T(8,128)}), f32[4,1,32,32,128]{4,3,2,1,0:T(8,128)}) %all-gather.3.cloned.1.call-update) | async-done | bytes 2097168 | tf_op jit(solution)/shard_map/all_gather | solution.py:97
  198.3 1.9 reduce_sum.9
  200.2 0.8 broadcast_multiply_fusion
  (40 shorter events, 0.1 us)
Async XLA Ops:
  7.2 191.1 %all-gather.3.cloned.1.call-start = ((), (), s32[]{:S(2)}) async-start(), calls=%async_computation | async-start | bytes 2621440 | tf_op jit(solution)/shard_map/all_gather | solution.py:97
  8.1 11.6 %collective-permute-start.1 = (f32[1,4,1,32,128]{4,3,2,1,0:T(8,128)S(1)}, f32[1,4,1,32,128]{4,3,2,1,0:T(8,128)S(1)}, u32[]{:S(2)}, u32[]{:S(2)}) collective-permute-start(f32[1,4,1,32,128]{4,3,2,1,0:T(8,128)S(1)} %get-tuple-element.39), channel_id=1, source_target_pairs={{0,2},{2,4},{4,6},{6,8},{8,10},{10,12},{12,14},{14,16},{16,18},{18... | collective-permute-start | bytes 196616 | tf_op jit(solution)/shard_map/ppermute | solution.py:15
  12.1 7.6 %copy-start.2 = (f32[1,4,32,32,128]{4,3,2,1,0:T(8,128)S(1)}, f32[1,4,32,32,128]{4,3,2,1,0:T(8,128)}, u32[]{:S(2)}) copy-start(f32[1,4,32,32,128]{4,3,2,1,0:T(8,128)} %param.8) | copy-start | bytes 6291460
  12.2 7.9 %collective-permute-start = (f32[1,4,1,32,128]{4,3,2,1,0:T(8,128)S(1)}, f32[1,4,1,32,128]{4,3,2,1,0:T(8,128)S(1)}, u32[]{:S(2)}, u32[]{:S(2)}) collective-permute-start(f32[1,4,1,32,128]{4,3,2,1,0:T(8,128)S(1)} %get-tuple-element.38), channel_id=1, source_target_pairs={{2,0},{4,2},{6,4},{8,6},{10,8},{12,10},{14,12},{16,14},{18,16},{20... | collective-permute-start | bytes 196616 | tf_op jit(solution)/shard_map/ppermute | solution.py:18
  19.7 10.0 %copy-start.3 = (f32[32,32,128]{2,1,0:T(8,128)}, f32[32,32,128]{2,1,0:T(8,128)S(1)}, u32[]{:S(2)}) copy-start(f32[32,32,128]{2,1,0:T(8,128)S(1)} %get-tuple-element.40) | copy-start | bytes 1572868
  19.7 10.0 %copy-start.4 = (f32[32,32,128]{2,1,0:T(8,128)}, f32[32,32,128]{2,1,0:T(8,128)S(1)}, u32[]{:S(2)}) copy-start(f32[32,32,128]{2,1,0:T(8,128)S(1)} %get-tuple-element.41) | copy-start | bytes 1572868
  19.7 10.0 %copy-start.5 = (f32[32,32,128]{2,1,0:T(8,128)}, f32[32,32,128]{2,1,0:T(8,128)S(1)}, u32[]{:S(2)}) copy-start(f32[32,32,128]{2,1,0:T(8,128)S(1)} %get-tuple-element.42) | copy-start | bytes 1572868
  19.7 10.0 %copy-start.6 = (f32[32,32,128]{2,1,0:T(8,128)}, f32[32,32,128]{2,1,0:T(8,128)S(1)}, u32[]{:S(2)}) copy-start(f32[32,32,128]{2,1,0:T(8,128)S(1)} %get-tuple-element.43) | copy-start | bytes 1572868
  19.7 10.0 %copy-start.7 = (f32[32,32,128]{2,1,0:T(8,128)}, f32[32,32,128]{2,1,0:T(8,128)S(1)}, u32[]{:S(2)}) copy-start(f32[32,32,128]{2,1,0:T(8,128)S(1)} %get-tuple-element.44) | copy-start | bytes 1572868
  19.7 10.0 %copy-start.8 = (f32[32,32,128]{2,1,0:T(8,128)}, f32[32,32,128]{2,1,0:T(8,128)S(1)}, u32[]{:S(2)}) copy-start(f32[32,32,128]{2,1,0:T(8,128)S(1)} %get-tuple-element.45) | copy-start | bytes 1572868
  19.8 5.8 %copy-start.13 = (f32[32,32,128]{2,1,0:T(8,128)S(1)}, f32[32,32,128]{2,1,0:T(8,128)}, u32[]{:S(2)}) copy-start(f32[32,32,128]{2,1,0:T(8,128)} %param.12) | copy-start | bytes 1572868
  19.8 5.8 %copy-start.14 = (f32[32,32,128]{2,1,0:T(8,128)S(1)}, f32[32,32,128]{2,1,0:T(8,128)}, u32[]{:S(2)}) copy-start(f32[32,32,128]{2,1,0:T(8,128)} %param.11) | copy-start | bytes 1572868
  20.1 5.7 %collective-permute-start.2 = (f32[1,4,34,1,128]{4,3,2,1,0:T(1,128)S(1)}, f32[1,4,34,1,128]{4,3,2,1,0:T(1,128)S(1)}, u32[]{:S(2)}, u32[]{:S(2)}) collective-permute-start(f32[1,4,34,1,128]{4,3,2,1,0:T(1,128)S(1)} %get-tuple-element.31), channel_id=1, source_target_pairs={{1,0},{3,2},{5,4},{7,6},{9,8},{11,10},{13,12},{15,14},{17,16},{19,... | collective-permute-start | bytes 208904 | tf_op jit(solution)/shard_map/ppermute | solution.py:18
  21.6 5.3 %collective-permute-start.3 = (f32[1,4,34,1,128]{4,3,2,1,0:T(1,128)S(1)}, f32[1,4,34,1,128]{4,3,2,1,0:T(1,128)S(1)}, u32[]{:S(2)}, u32[]{:S(2)}) collective-permute-start(f32[1,4,34,1,128]{4,3,2,1,0:T(1,128)S(1)} %get-tuple-element.30), channel_id=1, source_target_pairs={{0,1},{2,3},{4,5},{6,7},{8,9},{10,11},{12,13},{14,15},{16,17},{18,... | collective-permute-start | bytes 208904 | tf_op jit(solution)/shard_map/ppermute | solution.py:15
  25.8 12.4 %copy-start.9 = (f32[32,32,128]{2,1,0:T(8,128)}, f32[32,32,128]{2,1,0:T(8,128)S(1)}, u32[]{:S(2)}) copy-start(f32[32,32,128]{2,1,0:T(8,128)S(1)} %get-tuple-element.46) | copy-start | bytes 1572868
  25.8 12.4 %copy-start.10 = (f32[32,32,128]{2,1,0:T(8,128)}, f32[32,32,128]{2,1,0:T(8,128)S(1)}, u32[]{:S(2)}) copy-start(f32[32,32,128]{2,1,0:T(8,128)S(1)} %get-tuple-element.47) | copy-start | bytes 1572868
  29.7 8.5 %copy-start.11 = (f32[32,32,128]{2,1,0:T(8,128)S(1)}, f32[32,32,128]{2,1,0:T(8,128)}, u32[]{:S(2)}) copy-start(f32[32,32,128]{2,1,0:T(8,128)} %param.10) | copy-start | bytes 1572868
  41.2 5.9 %collective-permute-start.4 = (f32[1,4,1,32,128]{4,3,2,1,0:T(8,128)S(1)}, f32[1,4,1,32,128]{4,3,2,1,0:T(8,128)S(1)}, u32[]{:S(2)}, u32[]{:S(2)}) collective-permute-start(f32[1,4,1,32,128]{4,3,2,1,0:T(8,128)S(1)} %get-tuple-element.36), channel_id=1, source_target_pairs={{2,0},{4,2},{6,4},{8,6},{10,8},{12,10},{14,12},{16,14},{18,16},{20... | collective-permute-start | bytes 196616 | tf_op jit(solution)/shard_map/ppermute | solution.py:18
  42.5 5.9 %collective-permute-start.5 = (f32[1,4,1,32,128]{4,3,2,1,0:T(8,128)S(1)}, f32[1,4,1,32,128]{4,3,2,1,0:T(8,128)S(1)}, u32[]{:S(2)}, u32[]{:S(2)}) collective-permute-start(f32[1,4,1,32,128]{4,3,2,1,0:T(8,128)S(1)} %get-tuple-element.37), channel_id=1, source_target_pairs={{0,2},{2,4},{4,6},{6,8},{8,10},{10,12},{12,14},{14,16},{16,18},{18... | collective-permute-start | bytes 196616 | tf_op jit(solution)/shard_map/ppermute | solution.py:15
  48.5 5.5 %collective-permute-start.6 = (f32[1,4,34,1,128]{4,3,2,1,0:T(1,128)S(1)}, f32[1,4,34,1,128]{4,3,2,1,0:T(1,128)S(1)}, u32[]{:S(2)}, u32[]{:S(2)}) collective-permute-start(f32[1,4,34,1,128]{4,3,2,1,0:T(1,128)S(1)} %get-tuple-element.28), channel_id=1, source_target_pairs={{1,0},{3,2},{5,4},{7,6},{9,8},{11,10},{13,12},{15,14},{17,16},{19,... | collective-permute-start | bytes 208904 | tf_op jit(solution)/shard_map/ppermute | solution.py:18
  49.8 5.3 %collective-permute-start.7 = (f32[1,4,34,1,128]{4,3,2,1,0:T(1,128)S(1)}, f32[1,4,34,1,128]{4,3,2,1,0:T(1,128)S(1)}, u32[]{:S(2)}, u32[]{:S(2)}) collective-permute-start(f32[1,4,34,1,128]{4,3,2,1,0:T(1,128)S(1)} %get-tuple-element.29), channel_id=1, source_target_pairs={{0,1},{2,3},{4,5},{6,7},{8,9},{10,11},{12,13},{14,15},{16,17},{18,... | collective-permute-start | bytes 208904 | tf_op jit(solution)/shard_map/ppermute | solution.py:15
  76.3 5.6 %collective-permute-start.8 = (f32[1,4,1,32,128]{4,3,2,1,0:T(8,128)S(1)}, f32[1,4,1,32,128]{4,3,2,1,0:T(8,128)S(1)}, u32[]{:S(2)}, u32[]{:S(2)}) collective-permute-start(f32[1,4,1,32,128]{4,3,2,1,0:T(8,128)S(1)} %get-tuple-element.34), channel_id=1, source_target_pairs={{2,0},{4,2},{6,4},{8,6},{10,8},{12,10},{14,12},{16,14},{18,16},{20... | collective-permute-start | bytes 196616 | tf_op jit(solution)/shard_map/ppermute | solution.py:18
  77.6 5.6 %collective-permute-start.9 = (f32[1,4,1,32,128]{4,3,2,1,0:T(8,128)S(1)}, f32[1,4,1,32,128]{4,3,2,1,0:T(8,128)S(1)}, u32[]{:S(2)}, u32[]{:S(2)}) collective-permute-start(f32[1,4,1,32,128]{4,3,2,1,0:T(8,128)S(1)} %get-tuple-element.35), channel_id=1, source_target_pairs={{0,2},{2,4},{4,6},{6,8},{8,10},{10,12},{12,14},{14,16},{16,18},{18... | collective-permute-start | bytes 196616 | tf_op jit(solution)/shard_map/ppermute | solution.py:15
  83.3 5.3 %collective-permute-start.10 = (f32[1,4,34,1,128]{4,3,2,1,0:T(1,128)S(1)}, f32[1,4,34,1,128]{4,3,2,1,0:T(1,128)S(1)}, u32[]{:S(2)}, u32[]{:S(2)}) collective-permute-start(f32[1,4,34,1,128]{4,3,2,1,0:T(1,128)S(1)} %get-tuple-element.24), channel_id=1, source_target_pairs={{1,0},{3,2},{5,4},{7,6},{9,8},{11,10},{13,12},{15,14},{17,16},{19,... | collective-permute-start | bytes 208904 | tf_op jit(solution)/shard_map/ppermute | solution.py:18
  84.6 5.3 %collective-permute-start.11 = (f32[1,4,34,1,128]{4,3,2,1,0:T(1,128)S(1)}, f32[1,4,34,1,128]{4,3,2,1,0:T(1,128)S(1)}, u32[]{:S(2)}, u32[]{:S(2)}) collective-permute-start(f32[1,4,34,1,128]{4,3,2,1,0:T(1,128)S(1)} %get-tuple-element.25), channel_id=1, source_target_pairs={{0,1},{2,3},{4,5},{6,7},{8,9},{10,11},{12,13},{14,15},{16,17},{18,... | collective-permute-start | bytes 208904 | tf_op jit(solution)/shard_map/ppermute | solution.py:15
  111.1 17.5 %copy-start = (f32[1,2,2,32,32,128]{5,4,3,2,1,0:T(8,128)}, f32[1,2,2,32,32,128]{5,4,3,2,1,0:T(8,128)S(1)}, u32[]{:S(2)}) copy-start(f32[1,2,2,32,32,128]{5,4,3,2,1,0:T(8,128)S(1)} %copy.19) | copy-start | bytes 6291460
  111.1 5.9 %collective-permute-start.12 = (f32[1,4,1,32,128]{4,3,2,1,0:T(8,128)S(1)}, f32[1,4,1,32,128]{4,3,2,1,0:T(8,128)S(1)}, u32[]{:S(2)}, u32[]{:S(2)}) collective-permute-start(f32[1,4,1,32,128]{4,3,2,1,0:T(8,128)S(1)} %get-tuple-element.32), channel_id=1, source_target_pairs={{2,0},{4,2},{6,4},{8,6},{10,8},{12,10},{14,12},{16,14},{18,16},{20... | collective-permute-start | bytes 196616 | tf_op jit(solution)/shard_map/ppermute | solution.py:18
  112.4 5.9 %collective-permute-start.13 = (f32[1,4,1,32,128]{4,3,2,1,0:T(8,128)S(1)}, f32[1,4,1,32,128]{4,3,2,1,0:T(8,128)S(1)}, u32[]{:S(2)}, u32[]{:S(2)}) collective-permute-start(f32[1,4,1,32,128]{4,3,2,1,0:T(8,128)S(1)} %get-tuple-element.33), channel_id=1, source_target_pairs={{0,2},{2,4},{4,6},{6,8},{8,10},{10,12},{12,14},{14,16},{16,18},{18... | collective-permute-start | bytes 196616 | tf_op jit(solution)/shard_map/ppermute | solution.py:15
  118.4 5.9 %collective-permute-start.14 = (f32[1,4,34,1,128]{4,3,2,1,0:T(1,128)S(1)}, f32[1,4,34,1,128]{4,3,2,1,0:T(1,128)S(1)}, u32[]{:S(2)}, u32[]{:S(2)}) collective-permute-start(f32[1,4,34,1,128]{4,3,2,1,0:T(1,128)S(1)} %get-tuple-element.20), channel_id=1, source_target_pairs={{1,0},{3,2},{5,4},{7,6},{9,8},{11,10},{13,12},{15,14},{17,16},{19,... | collective-permute-start | bytes 208904 | tf_op jit(solution)/shard_map/ppermute | solution.py:18
  119.7 5.3 %collective-permute-start.15 = (f32[1,4,34,1,128]{4,3,2,1,0:T(1,128)S(1)}, f32[1,4,34,1,128]{4,3,2,1,0:T(1,128)S(1)}, u32[]{:S(2)}, u32[]{:S(2)}) collective-permute-start(f32[1,4,34,1,128]{4,3,2,1,0:T(1,128)S(1)} %get-tuple-element.21), channel_id=1, source_target_pairs={{0,1},{2,3},{4,5},{6,7},{8,9},{10,11},{12,13},{14,15},{16,17},{18,... | collective-permute-start | bytes 208904 | tf_op jit(solution)/shard_map/ppermute | solution.py:15
  148.5 2.3 %copy-start.1 = (f32[1,2,2,32,32,128]{5,4,3,2,1,0:T(8,128)S(1)}, f32[1,2,2,32,32,128]{5,4,3,2,1,0:T(8,128)}, u32[]{:S(2)}) copy-start(f32[1,2,2,32,32,128]{5,4,3,2,1,0:T(8,128)} %copy-done) | copy-start | bytes 6291460
  148.6 1.3 copy-start.12
Sparse Core Ops, SparseCore 0:
  152.2 46.0 all-gather.2
